TPU v7x, 512 devices: a whole 4x8x8 slice. The times are simulated.
512 devices in a mesh: gx: 16 (over x, z_hi), gy: 32 (over y, z_lo, core).
Axes of the slice: x: 4, y: 8, z: 8 (z_hi: 4, z_lo: 2; z = z_hi * 2 + z_lo), core: 2. Of those that a mesh axis runs over, the one named last changes fastest.
Arguments:
- prev_block: float32 [3, 8, 128, 256, 128], P(None, None, 'gx', 'gy'), may hold values from -20 to 20
- block: float32 [3, 8, 128, 256, 128], P(None, None, 'gx', 'gy'), may hold values from -20 to 20
- hop_seed: int32 [3, 128, 256, 128], P(None, 'gx', 'gy'), may hold values from 0 to 15
- levels: int32 [128, 256, 128], P('gx', 'gy'), may hold values from 0 to 15
- hop_table: float32 [3, 16, 3, 3], replicated, may hold values from -3 to 3
- onsite_table: float32 [16, 3], replicated, may hold values from -2 to 2
Outputs:
- next_block: float32 [3, 8, 128, 256, 128], P(None, None, 'gx', 'gy')
- alpha: float32 [8, 8], replicated
- beta: float32 [8, 8], replicated
All inputs are finite; a program needn't handle non-finite values.
Results may differ from a plain program's by a relative error of at most 0.0003.
Values sent between devices are 32-bit elements; how exact they have to be, the bound alone decides.
A program may use at most 64 MiB of HBM per device.

v0:
```python
import jax
import jax.numpy as jnp
from jax import lax
from jax.sharding import PartitionSpec as P

HIGH = lax.Precision.HIGHEST


def extended(value, sides, width):
    for axis, dim in sides:
        count, length = (lax.axis_size(axis), value.shape[dim])
        up = [(i, (i + 1) % count) for i in range(count)]
        down = [(j, i) for i, j in up]
        last = lax.slice_in_dim(value, length - width, length, axis=dim)
        leading = lax.slice_in_dim(value, 0, width, axis=dim)
        before = lax.ppermute(last, axis, up)
        after = lax.ppermute(leading, axis, down)
        value = jnp.concatenate([before, value, after], axis=dim)
    return value


def passed_along(value, axis, steps):
    count = lax.axis_size(axis)
    pairs = [(source, (source + steps) % count) for source in range(count)]
    return lax.ppermute(value, axis, pairs)


def table_rows(table_flat, indices):
    entries = table_flat.shape[0]
    flat = indices.reshape(-1)
    onehot = (flat[None, :] == jnp.arange(entries, dtype=jnp.int32)[:, None]).astype(jnp.float32)
    picked = lax.dot_general(table_flat, onehot, (((0,), (0,)), ((), ())), precision=HIGH)
    return picked.reshape((table_flat.shape[1],) + indices.shape)


def hop_blocks(table_dir, seeds):
    orbs = table_dir.shape[1]
    picked = table_rows(table_dir.reshape(table_dir.shape[0], orbs * orbs), seeds)
    return picked.reshape((orbs, orbs) + seeds.shape)


def forward(bonds, field):
    orbs = field.shape[0]
    rows = []
    for left in range(orbs):
        acc = bonds[left, 0][None] * field[0]
        for right in range(1, orbs):
            acc = acc + bonds[left, right][None] * field[right]
        rows.append(acc)
    return jnp.stack(rows, axis=0)


def backward(bonds, field):
    orbs = field.shape[0]
    rows = []
    for right in range(orbs):
        acc = bonds[0, right][None] * field[0]
        for left in range(1, orbs):
            acc = acc + bonds[left, right][None] * field[left]
        rows.append(acc)
    return jnp.stack(rows, axis=0)


def onsite_image(block, levels, onsite_table):
    energy = table_rows(onsite_table, levels)
    return energy[:, None] * block


def apply_values(block, hop_seed, levels, hop_table, onsite_table):
    padded = extended(block, (("gx", 2), ("gy", 3)), 1)
    ahead = [padded[:, :, 2:, 1:-1], padded[:, :, 1:-1, 2:], jnp.roll(block, -1, axis=4)]
    behind = [padded[:, :, :-2, 1:-1], padded[:, :, 1:-1, :-2], jnp.roll(block, 1, axis=4)]
    edge_x = passed_along(hop_seed[0, -1:], "gx", 1)
    edge_y = passed_along(hop_seed[1, :, -1:], "gy", 1)
    seeds_behind = [
        jnp.concatenate([edge_x, hop_seed[0, :-1]], axis=0),
        jnp.concatenate([edge_y, hop_seed[1, :, :-1]], axis=1),
        jnp.roll(hop_seed[2], 1, axis=2),
    ]
    image = onsite_image(block, levels, onsite_table)
    for direction in range(3):
        image = image + forward(
            hop_blocks(hop_table[direction], hop_seed[direction]), ahead[direction]
        )
        image = image + backward(
            hop_blocks(hop_table[direction], seeds_behind[direction]), behind[direction]
        )
    return image


def local_inner(left, right):
    total = None
    for orbit in range(left.shape[0]):
        flat_left = left[orbit].reshape(left.shape[1], -1)
        flat_right = right[orbit].reshape(right.shape[1], -1)
        part_sum = lax.dot_general(flat_left, flat_right, (((1,), (1,)), ((), ())), precision=HIGH)
        total = part_sum if total is None else total + part_sum
    return total


def apply_left(matrix, field):
    rows = []
    for orbit in range(field.shape[0]):
        flat = field[orbit].reshape(field.shape[1], -1)
        mixed = jnp.dot(matrix, flat, precision=HIGH)
        rows.append(mixed.reshape((matrix.shape[0],) + field.shape[2:]))
    return jnp.stack(rows, axis=0)


def combine(basis, coeffs):
    return apply_left(coeffs.T, basis)


def per_device(prev_block, block, hop_seed, levels, hop_table, onsite_table):
    count = (
        block.shape[0]
        * block.shape[2]
        * block.shape[3]
        * block.shape[4]
        * lax.axis_size("gx")
        * lax.axis_size("gy")
    )
    product = apply_values(block, hop_seed, levels, hop_table, onsite_table)
    basis = jnp.concatenate([prev_block, block], axis=1)
    width = block.shape[1]
    first = lax.psum(local_inner(basis, product), ("gx", "gy")) / count
    residual_one = product - combine(basis, first)
    second = lax.psum(local_inner(basis, residual_one), ("gx", "gy")) / count
    residual_two = residual_one - combine(basis, second)
    gram = lax.psum(local_inner(residual_two, residual_two), ("gx", "gy")) / count
    alpha = first[width:]
    lower = jnp.linalg.cholesky(gram)
    lower_inv = jax.scipy.linalg.solve_triangular(
        lower, jnp.eye(width, dtype=jnp.float32), lower=True
    )
    next_block = apply_left(lower_inv, residual_two)
    return (next_block, alpha, lower.T)


def solution(mesh):
    in_specs = (
        P(None, None, "gx", "gy", None),
        P(None, None, "gx", "gy", None),
        P(None, "gx", "gy", None),
        P("gx", "gy", None),
        P(),
        P(),
    )
    out_specs = (P(None, None, "gx", "gy", None), P(), P())
    return jax.shard_map(
        per_device, mesh=mesh, in_specs=in_specs, out_specs=out_specs, check_vma=False
    )
```

profile of v0, /device:TPU:1, one launch (start us, length us, event | category | flops | bytes accessed | tf_op | source)
XLA Modules:
  0.0 391.7 jit_solution(6826044836774343264)
XLA Ops:
  0.7 1.0 fusion.80
  1.7 0.7 copy.105
  2.3 6.6 %collective-permute-start.2 = (f32[3,8,1,8,128]{4,1,3,2,0:T(8,128)}, f32[3,8,1,8,128]{4,1,3,2,0:T(8,128)}, u32[]{:S(2)}, u32[]{:S(2)}) collective-permute-start(f32[3,8,1,8,128]{4,1,3,2,0:T(8,128)} %copy.105), channel_id=1, source_target_pairs={{0,32},{32,64},{64,96},{96,128},{128,160},{160,192},{192,224},{224... | collective-permute-start | bytes 294920 | tf_op jit(solution)/shard_map/ppermute | solution.py:16
  9.0 0.7 copy.104
  9.6 9.0 %collective-permute-start = (f32[3,8,1,8,128]{4,1,3,2,0:T(8,128)}, f32[3,8,1,8,128]{4,1,3,2,0:T(8,128)}, u32[]{:S(2)}, u32[]{:S(2)}) collective-permute-start(f32[3,8,1,8,128]{4,1,3,2,0:T(8,128)} %copy.104), channel_id=1, source_target_pairs={{32,0},{64,32},{96,64},{128,96},{160,128},{192,160},{224,192},{256... | collective-permute-start | bytes 294920 | tf_op jit(solution)/shard_map/ppermute | solution.py:17
  18.6 1.4 slice.453
  20.0 3.9 %collective-permute-start.4 = (s32[8,1,128]{2,0,1:T(8,128)}, s32[8,1,128]{2,0,1:T(8,128)}, u32[]{:S(2)}, u32[]{:S(2)}) collective-permute-start(s32[8,1,128]{2,0,1:T(8,128)} %bitcast.37), channel_id=1, source_target_pairs={{0,1},{1,2},{2,3},{3,4},{4,5},{5,6},{6,7},{7,8},{8,9},{9,10},{10,1... | collective-permute-start | bytes 12296 | tf_op jit(solution)/shard_map/ppermute | solution.py:25
  23.9 1.3 slice_bitcast_fusion.72
  25.2 1.9 collective-permute-start.1
  27.1 0.8 slice_bitcast_fusion.69
  27.9 1.1 fusion.79
  29.1 1.2 fusion.78
  32.2 0.7 slice_bitcast_fusion.17
  32.9 1.6 copy.108
  34.5 1.3 copy.109
  36.3 0.7 slice_bitcast_fusion.26
  37.0 1.4 copy.106
  38.4 1.3 copy.107
  40.7 0.7 slice_bitcast_fusion.44
  42.6 1.8 multiply_add_fusion.2
  44.5 1.4 multiply_add_fusion.1
  46.0 1.1 multiply_add_fusion.4
  47.5 0.7 add_bitcast_fusion.1
  48.7 0.7 slice_bitcast_fusion.35
  49.9 0.9 constant_dynamic-update-slice_fusion.6
  51.4 0.9 constant_dynamic-update-slice_fusion.4
  52.3 0.7 fusion.77
  53.1 1.9 collective-permute-start.3
  55.0 3.8 collective-permute-start.5
  58.8 1.1 fusion.76
  60.0 1.1 multiply_add_fusion.17
  61.0 1.0 multiply_add_fusion.14
  62.4 1.2 copy.45
  63.6 0.9 reshape_squeeze.22
  64.5 1.1 copy.83
  65.7 2.0 copy.47
  67.7 1.9 reshape_squeeze.23
  69.6 2.0 copy.84
  71.8 1.2 multiply_add_fusion.8
  75.3 0.9 fusion.10
  76.3 0.7 convolution_bitcast_fusion.16
  77.0 0.8 fusion.3
  77.8 0.8 fusion.2
  78.6 101.8 %psum.21 = f32[16,8]{0,1:T(8,128)S(1)} all-reduce(f32[16,8]{0,1:T(8,128)S(1)} %fusion.2), channel_id=1, replica_groups=mesh['gx'=16,'gy'=32] {'gx','gy'}, use_global_device_ids=true, to_apply=%region_0.1 | all-reduce | flops 128 | bytes 1024 | tf_op jit(solution)/shard_map/psum | solution.py:126
  180.4 0.7 convolution_bitcast_fusion.5
  181.1 0.7 convolution_bitcast_fusion.4
  181.8 0.7 convolution_bitcast_fusion.3
  182.5 2.7 maximum_subtract_fusion
  185.3 0.7 convolution_bitcast_fusion.13
  186.0 0.8 fusion.1
  186.8 0.8 fusion
  187.6 94.6 %psum.22 = f32[16,8]{0,1:T(8,128)S(1)} all-reduce(f32[16,8]{0,1:T(8,128)S(1)} %fusion), channel_id=1, replica_groups=mesh['gx'=16,'gy'=32] {'gx','gy'}, use_global_device_ids=true, to_apply=%region_1.2 | all-reduce | flops 128 | bytes 1024 | tf_op jit(solution)/shard_map/psum | solution.py:128
  282.2 0.6 convolution_bitcast_fusion.2
  282.9 0.7 convolution_bitcast_fusion.1
  283.6 1.7 convolution_bitcast_fusion
  285.3 3.5 maximum_subtract_fusion.1
  288.7 0.7 convolution_bitcast_fusion.17
  289.4 0.7 convolution_bitcast_fusion.18
  290.1 0.7 fusion.5
  290.8 94.3 %psum.23 = f32[8,8]{0,1:T(8,128)S(1)} all-reduce(f32[8,8]{0,1:T(8,128)S(1)} %fusion.5), channel_id=1, replica_groups=mesh['gx'=16,'gy'=32] {'gx','gy'}, use_global_device_ids=true, to_apply=%region_2.3 | all-reduce | flops 64 | bytes 512 | tf_op jit(solution)/shard_map/psum | solution.py:130
  385.2 0.7 cholesky.17
  389.3 1.0 copy.57
  390.3 0.7 copy.59
  391.0 0.7 copy.58
  (201 shorter events, 12.2 us)
Async XLA Ops:
  0.6 46.5 %copy-start = (f32[16,3]{0,1:T(4,128)S(1)}, f32[16,3]{0,1:T(4,128)}, u32[]{:S(2)}) copy-start(f32[16,3]{0,1:T(4,128)} %param.11) | copy-start | bytes 580
  0.6 27.3 %copy-start.1 = (f32[3,8,8,8,128]{4,3,2,1,0:T(8,128)S(1)}, f32[3,8,8,8,128]{4,3,2,1,0:T(8,128)}, u32[]{:S(2)}) copy-start(f32[3,8,8,8,128]{4,3,2,1,0:T(8,128)} %param.7) | copy-start | bytes 2359300
  2.3 47.6 %collective-permute-start.2 = (f32[3,8,1,8,128]{4,1,3,2,0:T(8,128)}, f32[3,8,1,8,128]{4,1,3,2,0:T(8,128)}, u32[]{:S(2)}, u32[]{:S(2)}) collective-permute-start(f32[3,8,1,8,128]{4,1,3,2,0:T(8,128)} %copy.105), channel_id=1, source_target_pairs={{0,32},{32,64},{64,96},{96,128},{128,160},{160,192},{192,224},{224... | collective-permute-start | bytes 294920 | tf_op jit(solution)/shard_map/ppermute | solution.py:16
  9.6 41.8 %collective-permute-start = (f32[3,8,1,8,128]{4,1,3,2,0:T(8,128)}, f32[3,8,1,8,128]{4,1,3,2,0:T(8,128)}, u32[]{:S(2)}, u32[]{:S(2)}) collective-permute-start(f32[3,8,1,8,128]{4,1,3,2,0:T(8,128)} %copy.104), channel_id=1, source_target_pairs={{32,0},{64,32},{96,64},{128,96},{160,128},{192,160},{224,192},{256... | collective-permute-start | bytes 294920 | tf_op jit(solution)/shard_map/ppermute | solution.py:17
  20.0 27.5 %collective-permute-start.4 = (s32[8,1,128]{2,0,1:T(8,128)}, s32[8,1,128]{2,0,1:T(8,128)}, u32[]{:S(2)}, u32[]{:S(2)}) collective-permute-start(s32[8,1,128]{2,0,1:T(8,128)} %bitcast.37), channel_id=1, source_target_pairs={{0,1},{1,2},{2,3},{3,4},{4,5},{5,6},{6,7},{7,8},{8,9},{9,10},{10,1... | collective-permute-start | bytes 12296 | tf_op jit(solution)/shard_map/ppermute | solution.py:25
  25.2 24.2 %collective-permute-start.1 = (s32[1,8,128]{2,1,0:T(8,128)}, s32[1,8,128]{2,1,0:T(8,128)S(1)}, u32[]{:S(2)}, u32[]{:S(2)}) collective-permute-start(s32[1,8,128]{2,1,0:T(8,128)} %slice_bitcast_fusion.72), channel_id=1, source_target_pairs={{0,32},{32,64},{64,96},{96,128},{128,160},{160,192},{192,224},{224... | collective-permute-start | bytes 12296 | tf_op jit(solution)/shard_map/ppermute | solution.py:25
  29.1 2.5 copy-start.71
  32.1 2.3 copy-start.34
  37.0 2.7 copy-start.40
  40.2 1.6 copy-start.68
  41.9 2.5 copy-start.3
  41.9 2.4 copy-start.4
  41.9 2.4 copy-start.54
  42.0 2.4 copy-start.55
  42.0 2.4 copy-start.56
  42.0 2.4 copy-start.63
  42.0 2.4 copy-start.64
  42.0 2.4 copy-start.65
  44.4 1.5 copy-start.57
  44.4 1.5 copy-start.58
  44.5 1.5 copy-start.59
  44.5 1.5 copy-start.60
  44.5 1.5 copy-start.61
  44.5 1.5 copy-start.62
  45.9 1.5 copy-start.66
  45.9 2.2 copy-start.69
  47.4 2.0 copy-start.67
  52.3 7.6 %copy-start.38 = (f32[3,8,10,8,128]{4,1,3,2,0:T(8,128)}, f32[3,8,10,8,128]{4,1,3,2,0:T(8,128)S(1)}, u32[]{:S(2)}) copy-start(f32[3,8,10,8,128]{4,1,3,2,0:T(8,128)S(1)} %get-tuple-element.112) | copy-start | bytes 2949124
  53.1 18.6 %collective-permute-start.3 = (f32[3,8,10,1,128]{4,1,3,2,0:T(8,128)}, f32[3,8,10,1,128]{4,1,3,2,0:T(8,128)}, u32[]{:S(2)}, u32[]{:S(2)}) collective-permute-start(f32[3,8,10,1,128]{4,1,3,2,0:T(8,128)} %get-tuple-element.33), channel_id=1, source_target_pairs={{1,0},{2,1},{3,2},{4,3},{5,4},{6,5},{7,6},{8,7},{9,8},{10,9},{11,1... | collective-permute-start | bytes 368648 | tf_op jit(solution)/shard_map/ppermute | solution.py:17
  55.0 16.7 %collective-permute-start.5 = (f32[3,8,10,1,128]{4,1,3,2,0:T(8,128)}, f32[3,8,10,1,128]{4,1,3,2,0:T(8,128)}, u32[]{:S(2)}, u32[]{:S(2)}) collective-permute-start(f32[3,8,10,1,128]{4,1,3,2,0:T(8,128)} %get-tuple-element.32), channel_id=1, source_target_pairs={{0,1},{1,2},{2,3},{3,4},{4,5},{5,6},{6,7},{7,8},{8,9},{9,10},{10,1... | collective-permute-start | bytes 368648 | tf_op jit(solution)/shard_map/ppermute | solution.py:16
  69.6 2.0 copy-start.39
  71.7 1.5 copy-start.42
  71.7 1.5 copy-start.43
  71.7 1.5 copy-start.44
  71.7 1.5 copy-start.45
  71.7 1.5 copy-start.46
  71.7 1.5 copy-start.47
  71.8 1.8 copy-start.27
  73.0 3.3 copy-start.28
  73.0 3.3 copy-start.29
  73.1 1.5 copy-start.17
  73.1 1.8 copy-start.19
  73.1 1.9 copy-start.21
  73.1 2.0 copy-start.23
  73.1 2.1 copy-start.24
  73.1 2.1 copy-start.25
  73.1 2.2 copy-start.26
  73.5 2.7 copy-start.30
  73.6 2.7 copy-start.31
  73.6 2.7 copy-start.32
  73.6 2.7 copy-start.33
  180.4 2.1 copy-start.7
  180.4 2.1 copy-start.10
  180.4 2.1 copy-start.13
  180.4 2.1 copy-start.16
  180.4 2.1 copy-start.18
  180.4 2.1 copy-start.20
  180.4 2.1 copy-start.22
  181.1 4.2 %copy-start.35 = (f32[1,8,8,8,128]{4,1,3,2,0:T(8,128)}, f32[1,8,8,8,128]{4,1,3,2,0:T(8,128)S(1)}, u32[]{:S(2)}) copy-start(f32[1,8,8,8,128]{4,1,3,2,0:T(8,128)S(1)} %convolution_bitcast_fusion.5) | copy-start | bytes 786436
  181.8 3.5 copy-start.36
  182.5 2.8 copy-start.37
  187.6 97.7 %copy-start.8 = (f32[1,8,8,8,128]{4,1,3,2,0:T(8,128)S(1)}, f32[1,8,8,8,128]{4,1,3,2,0:T(8,128)}, u32[]{:S(2)}) copy-start(f32[1,8,8,8,128]{4,1,3,2,0:T(8,128)} %get-tuple-element.9) | copy-start | bytes 786436
  187.6 97.7 %copy-start.11 = (f32[1,8,8,8,128]{4,1,3,2,0:T(8,128)S(1)}, f32[1,8,8,8,128]{4,1,3,2,0:T(8,128)}, u32[]{:S(2)}) copy-start(f32[1,8,8,8,128]{4,1,3,2,0:T(8,128)} %get-tuple-element.21) | copy-start | bytes 786436
  187.6 97.7 %copy-start.14 = (f32[1,8,8,8,128]{4,1,3,2,0:T(8,128)S(1)}, f32[1,8,8,8,128]{4,1,3,2,0:T(8,128)}, u32[]{:S(2)}) copy-start(f32[1,8,8,8,128]{4,1,3,2,0:T(8,128)} %get-tuple-element.22) | copy-start | bytes 786436
  (14 other events, 18.8 us)
where the time goes:
time: 393 us; the launch traced here: 392 us
  blocking collectives  291 us (74%)
  local copies, waits for them, and re-layouts  38 us (10%)
  starting transfers between devices  27.2 us (7%)
  other arithmetic  18.6 us (5%)
  matrix products  15.1 us (4%)
    psum x1, blocking collectives, per_device(): first = lax.psum(local_inner(basis, product), ('gx', 'gy')) / count  102 us
    psum x1, blocking collectives, per_device(): second = lax.psum(local_inner(basis, residual_one), ('gx', 'gy')) / count  94.6 us
    psum x1, blocking collectives, per_device(): lax.psum(local_inner(residual_two, residual_two), ('gx', 'gy')) / count  94.3 us
    unnamed x171, local copies, waits for them, and re-layouts  17.2 us
    ppermute x2, starting transfers between devices, extended(): after = lax.ppermute(leading, axis, down)  10.9 us
    ppermute x2, starting transfers between devices, extended(): before = lax.ppermute(last, axis, up)  10.5 us
  transfers between devices with their start and end apart: 6, of which 0 were waited for; matrix products, arithmetic and copies ran while one was open for 10% of the time, Pallas kernels for 0%

commit v1 on v0

v1 whole, which is shorter than its diff:
```python
import functools

import jax
import jax.numpy as jnp
from jax import lax
from jax.experimental import pallas as pl
from jax.experimental.pallas import tpu as pltpu
from jax.sharding import PartitionSpec as P

HIGH = lax.Precision.HIGHEST
MESH = pl.DeviceIdType.MESH
ORB, WIDTH, SIDE, LANES, KINDS = 3, 8, 8, 128, 16
ROWS = SIDE * SIDE
FIELDS = 3 * WIDTH

DIGITS = {"x": 4, "zh": 4, "y": 8, "zl": 2, "core": 2}
STAGES = (("core", "y"), ("x", "zh", "zl"))


def position():
    gx, gy = lax.axis_index("gx"), lax.axis_index("gy")
    return {"x": gx // 4, "zh": gx % 4, "y": gy // 4, "zl": (gy // 2) % 2, "core": gy % 2}


def device(pos):
    return (pos["x"] * 4 + pos["zh"], pos["y"] * 4 + pos["zl"] * 2 + pos["core"])


def group_size(dims):
    size = 1
    for dim in dims:
        size *= DIGITS[dim]
    return size


def member(pos, dims):
    index = 0
    for dim in dims:
        index = index * DIGITS[dim] + pos[dim]
    return index


def offsets(dims):
    found = []
    for k in range(1, group_size(dims)):
        off, rest = {}, k
        for dim in reversed(dims):
            off[dim] = rest % DIGITS[dim]
            rest //= DIGITS[dim]
        hops = 0
        if "y" in off:
            hops += min(off["y"], 8 - off["y"])
        if "x" in off:
            hops += min(off["x"], 4 - off["x"])
        if "zh" in off:
            z = (off["zh"] * 2 + off.get("zl", 0)) % 8
            hops += min(z, 8 - z)
        found.append((-hops, k, off))
    return [off for _, _, off in sorted(found, key=lambda t: t[:2])]


def peer(pos, off):
    return {d: (pos[d] + off[d]) % DIGITS[d] if off.get(d) else pos[d] for d in pos}


def iota(axis):
    return lax.broadcasted_iota(jnp.int32, (8, LANES), axis)


def fold_rows(parts):
    row = iota(0)
    for bit in (1, 2, 4):
        low = (row & bit) == 0
        parts = [
            jnp.where(low, a, b) + pltpu.roll(jnp.where(low, b, a), bit, axis=0)
            for a, b in zip(parts[0::2], parts[1::2])
        ]
    return parts[0]


def inner_rows(fields, first, others, lane, sums):
    def step(x, acc):
        rows = pl.ds(pl.multiple_of(8 * x + 8, 8), 8)
        for orb in range(ORB):
            left = [fields[orb, first + r, rows, :] for r in range(4)]
            right = [fields[orb, others + s, rows, :] for s in range(8)]
            acc = [acc[r * 8 + s] + left[r] * right[s] for r in range(4) for s in range(8)]
        return tuple(acc)

    zero = jnp.zeros((8, LANES), jnp.float32)
    acc = lax.fori_loop(0, SIDE, step, (zero,) * 32)
    for r in range(4):
        column = jnp.sum(fold_rows(list(acc[r * 8 : r * 8 + 8])), axis=1, keepdims=True)
        sums = jnp.where(iota(1) == lane + r, column, sums)
    return sums


def picked(table, index):
    return jnp.take_along_axis(table, index, axis=1, mode="promise_in_bounds")


def apply_and_reduce(
    nx, ny, prev, block, seeds, levels, hop, onsite, product, stats,
    fields, seed_v, level_v, hop_v, onsite_v, table, coef_x, coef_y, coef_z, energy,
    edge_y, halo_x, halo_y, seed_edge, seed_x, seed_y, slots_one, slots_two,
    load_sem, halo_send, halo_recv, sum_send, sum_recv, store_sem,
):
    gx, gy = lax.axis_index("gx"), lax.axis_index("gy")
    right, left = ((gx + 1) % nx, gy), ((gx + nx - 1) % nx, gy)
    above, below = (gx, (gy + 1) % ny), (gx, (gy + ny - 1) % ny)
    pos = position()
    plans = [offsets(dims) for dims in STAGES]

    barrier = pltpu.get_barrier_semaphore()
    partners = [right, left, above, below]
    partners += [device(peer(pos, off)) for plan in plans for off in plan]
    for partner in partners:
        pl.semaphore_signal(barrier, inc=1, device_id=partner, device_id_type=MESH)

    inside = pl.ds(8, ROWS)
    loads = [
        pltpu.make_async_copy(seeds, seed_v, load_sem.at[0]),
        pltpu.make_async_copy(block, fields.at[:, pl.ds(WIDTH, WIDTH), inside, :], load_sem.at[1]),
        pltpu.make_async_copy(hop, hop_v, load_sem.at[2]),
        pltpu.make_async_copy(onsite, onsite_v, load_sem.at[3]),
        pltpu.make_async_copy(levels, level_v, load_sem.at[4]),
        pltpu.make_async_copy(prev, fields.at[:, pl.ds(0, WIDTH), inside, :], load_sem.at[5]),
    ]
    for load in loads:
        load.start()

    pl.semaphore_wait(barrier, len(partners))

    def send(i, src, dst, to):
        return pltpu.make_async_remote_copy(
            src_ref=src, dst_ref=dst, send_sem=halo_send.at[i], recv_sem=halo_recv.at[i],
            device_id=to, device_id_type=MESH,
        )

    last, lead = pl.ds(ROWS - 8, 8), pl.ds(0, 8)
    sends = [
        send(0, seeds.at[0, last, :], seed_x, right),
        send(1, block.at[:, :, last, :], halo_x.at[0], right),
        send(2, block.at[:, :, lead, :], halo_x.at[1], left),
    ]
    for copy in sends:
        copy.start()
    loads[0].wait()
    seed_edge[...] = seed_v[1, pl.ds(7, 8, stride=8), :]
    loads[1].wait()

    def pack(n, _):
        for orb in range(ORB):
            edge_y[0, orb, n] = fields[orb, WIDTH + n, pl.ds(15, 8, stride=8), :]
            edge_y[1, orb, n] = fields[orb, WIDTH + n, pl.ds(8, 8, stride=8), :]
        return 0

    lax.fori_loop(0, WIDTH, pack, 0)
    more = [
        send(3, seed_edge, seed_y, above),
        send(4, edge_y.at[0], halo_y.at[0], above),
        send(5, edge_y.at[1], halo_y.at[1], below),
    ]
    for copy in more:
        copy.start()
    sends += more

    for load in loads[2:5]:
        load.wait()
    zero = jnp.zeros((8, LANES), jnp.float32)

    for a in range(ORB):
        table[27 + a, :, 0:KINDS] = jnp.broadcast_to(onsite_v[a : a + 1, :], (8, KINDS))
        for d in range(3):
            for b in range(ORB):
                table[d * 9 + a * 3 + b, :, 0:KINDS] = jnp.broadcast_to(hop_v[d, a, b : b + 1, :], (8, KINDS))

    for n in range(WIDTH):
        for orb in range(ORB):
            fields[orb, WIDTH + n, 0:8, :] = zero
            fields[orb, WIDTH + n, ROWS + 8 : ROWS + 16, :] = zero
    for ab in range(9):
        coef_x[ab, 0:8, :] = zero
    inner_row = iota(0) < 7

    def look_up(x, _):
        rows = pl.ds(pl.multiple_of(8 * x, 8), 8)
        later = pl.ds(pl.multiple_of(8 * x + 8, 8), 8)
        at_x, at_y, at_z = (seed_v[d, rows, :] for d in range(3))
        level = level_v[rows, :]
        for a in range(ORB):
            energy[a, rows, :] = picked(table[27 + a], level)
            for b in range(ORB):
                ab = a * 3 + b
                coef_x[ab, later, :] = picked(table[ab], at_x)
                coef_y[ab, rows, :] = jnp.where(inner_row, picked(table[9 + ab], at_y), 0.0)
                coef_z[ab, rows, :] = picked(table[18 + ab], at_z)
        return 0

    lax.fori_loop(0, SIDE, look_up, 0)

    def own(x, _):
        before = pl.ds(pl.multiple_of(8 * x, 8), 8)
        here = pl.ds(pl.multiple_of(8 * x + 8, 8), 8)
        after = pl.ds(pl.multiple_of(8 * x + 16, 8), 8)
        cx = [coef_x[ab, here, :] for ab in range(9)]
        cm = [coef_x[ab, before, :] for ab in range(9)]
        cy = [coef_y[ab, before, :] for ab in range(9)]
        cz = [coef_z[ab, before, :] for ab in range(9)]
        ce = [energy[a, before, :] for a in range(ORB)]
        for n in range(WIDTH):
            v = [fields[b, WIDTH + n, here, :] for b in range(ORB)]
            vp = [fields[b, WIDTH + n, after, :] for b in range(ORB)]
            vm = [fields[b, WIDTH + n, before, :] for b in range(ORB)]
            vz = [pltpu.roll(u, LANES - 1, axis=1) for u in v]
            vy = [pltpu.roll(u, 7, axis=0) for u in v]
            for a in range(ORB):
                carried_z = cz[a] * v[0] + cz[3 + a] * v[1] + cz[6 + a] * v[2]
                carried_y = cy[a] * v[0] + cy[3 + a] * v[1] + cy[6 + a] * v[2]
                out = ce[a] * v[a] + pltpu.roll(carried_z, 1, axis=1) + pltpu.roll(carried_y, 1, axis=0)
                for b in range(ORB):
                    out = out + cx[a * 3 + b] * vp[b] + cm[b * 3 + a] * vm[b]
                    out = out + cz[a * 3 + b] * vz[b] + cy[a * 3 + b] * vy[b]
                fields[a, 2 * WIDTH + n, here, :] = out
        return 0

    lax.fori_loop(0, SIDE, own, 0)

    loads[5].wait()

    def basis_rows(i, sums):
        sums = inner_rows(fields, 4 * i, 0, 32 + 4 * i, sums)
        return inner_rows(fields, 4 * i, WIDTH, 48 + 4 * i, sums)

    sums = lax.fori_loop(0, 4, basis_rows, zero)

    for copy in sends:
        copy.wait_recv()
    cm = [picked(table[ab], seed_x[...]) for ab in range(9)]
    cb = [picked(table[9 + ab], seed_y[...]) for ab in range(9)]
    cf = [picked(table[9 + ab], seed_edge[...]) for ab in range(9)]
    cp = [coef_x[ab, ROWS : ROWS + 8, :] for ab in range(9)]

    def edges(n, _):
        for a in range(ORB):
            field = fields.at[a, 2 * WIDTH + n]
            low, high = field[8:16, :], field[ROWS : ROWS + 8, :]
            for b in range(ORB):
                low = low + cm[b * 3 + a] * halo_x[0, b, n]
                high = high + cp[a * 3 + b] * halo_x[1, b, n]
            field[8:16, :] = low
            field[ROWS : ROWS + 8, :] = high
            low, high = field[pl.ds(8, 8, stride=8), :], field[pl.ds(15, 8, stride=8), :]
            for b in range(ORB):
                low = low + cb[b * 3 + a] * halo_y[0, b, n]
                high = high + cf[a * 3 + b] * halo_y[1, b, n]
            field[pl.ds(8, 8, stride=8), :] = low
            field[pl.ds(15, 8, stride=8), :] = high
        return 0

    lax.fori_loop(0, WIDTH, edges, 0)
    keep = pltpu.make_async_copy(fields.at[:, pl.ds(2 * WIDTH, WIDTH), inside, :], product, store_sem)
    keep.start()

    def product_rows(i, sums):
        return inner_rows(fields, 4 * i, 2 * WIDTH, 4 * i, sums)

    sums = lax.fori_loop(0, 6, product_rows, sums)
    value = (sums + pltpu.roll(pltpu.roll(sums, 4, axis=0), 64, axis=1))[0:4, :]
    for s, (dims, plan, slots) in enumerate(zip(STAGES, plans, (slots_one, slots_two))):
        me, size = member(pos, dims), group_size(dims)
        slots[me] = value
        for off in plan:
            pltpu.make_async_remote_copy(
                src_ref=slots.at[me], dst_ref=slots.at[me], send_sem=sum_send.at[s], recv_sem=sum_recv.at[s],
                device_id=device(peer(pos, off)), device_id_type=MESH,
            ).start()
        bulk = slots.at[pl.ds(0, size - 1)]
        pltpu.make_async_copy(bulk, bulk, sum_recv.at[s]).wait()
        value = slots[0]
        for k in range(1, size):
            value = value + slots[k]
    stats[...] = value
    for copy in sends:
        copy.wait_send()
    for s, (dims, slots) in enumerate(zip(STAGES, (slots_one, slots_two))):
        bulk = slots.at[pl.ds(0, group_size(dims) - 1)]
        pltpu.make_async_copy(bulk, bulk, sum_send.at[s]).wait()
    keep.wait()


def wide(matrix):
    return jnp.concatenate([matrix, jnp.zeros((LANES - matrix.shape[0], LANES), jnp.float32)], axis=0)


def rows_dot(left, right):
    return lax.dot_general(
        left, wide(right), (((1,), (1,)), ((), ())), precision=HIGH, preferred_element_type=jnp.float32
    )


def finish(
    count, prev, block, product, stats, out, alpha, beta,
    fields, result, columns, spread, load_sem, store_sem,
):
    loads = []
    for orb in range(ORB):
        for i, source in enumerate((prev, block, product)):
            target = fields.at[orb, pl.ds(i * WIDTH, WIDTH)]
            loads.append(pltpu.make_async_copy(source.at[orb], target, load_sem.at[orb, i]))
    for load in loads:
        load.start()
    row, lane = iota(0), iota(1)
    scaled = stats[...] * (1.0 / count)
    sums = jnp.concatenate([scaled, pltpu.roll(scaled, 64, axis=1)], axis=0)
    first = jnp.where(lane < 16, sums, 0.0)
    norms = jnp.where(lane < 8, pltpu.roll(sums, LANES - 16, axis=1), 0.0)
    metric = [jnp.where(lane < 16, pltpu.roll(sums, LANES - at, axis=1), 0.0) for at in (32, 48)]
    twice = [jnp.where(row + 8 * i == lane, 2.0, 0.0) - metric[i] for i in range(2)]
    metric, twice = (jnp.concatenate(m, axis=0) for m in (metric, twice))
    coeffs = rows_dot(first, twice)
    for k in range(2 * WIDTH):
        spread[k] = jnp.broadcast_to(coeffs[:, k : k + 1], (8, LANES))
    last = jnp.where(lane < 8, pltpu.roll(first, LANES - 8, axis=1), 0.0)
    unit = jnp.where(row == lane, 1.0, 0.0)
    alpha[...] = rows_dot(unit, last)[:, 0:WIDTH]
    gram = norms + rows_dot(rows_dot(coeffs, metric) - first, coeffs) - rows_dot(coeffs, first)
    for j in range(WIDTH):
        columns[j] = jnp.broadcast_to(gram[:, j : j + 1], (8, LANES))

    a = [[jnp.broadcast_to(columns[j, i : i + 1, :], (8, LANES)) for j in range(i + 1)] for i in range(WIDTH)]
    inverse = [[None] * WIDTH for _ in range(WIDTH)]
    upper = jnp.zeros((8, LANES), jnp.float32)
    for j in range(WIDTH):
        inverse[j][j] = lax.rsqrt(a[j][j])
        for i in range(j, WIDTH):
            a[i][j] = a[i][j] * inverse[j][j]
            upper = jnp.where((row == j) & (lane == i), a[i][j], upper)
        for i in range(j + 1, WIDTH):
            for k in range(j + 1, i + 1):
                a[i][k] = a[i][k] - a[i][j] * a[k][j]
    for i in range(WIDTH):
        for j in range(i):
            total = a[i][j] * inverse[j][j]
            for k in range(j + 1, i):
                total = total + a[i][k] * inverse[k][j]
            inverse[i][j] = -(total * inverse[i][i])
    beta[...] = upper[:, 0:WIDTH]
    for i in range(WIDTH):
        for j in range(i + 1):
            columns[WIDTH + i * WIDTH + j] = inverse[i][j]

    stores = []
    for orb in range(ORB):
        for load in loads[3 * orb : 3 * orb + 3]:
            load.wait()

        def rest(m, _):
            for half in range(2):
                tiles = [pl.ds(8 * (4 * half + x), 8) for x in range(4)]
                acc = [[fields[orb, 2 * WIDTH + 2 * m + r, t, :] for t in tiles] for r in range(2)]
                for k in range(2 * WIDTH):
                    c = [jnp.broadcast_to(spread[k, pl.ds(2 * m + r, 1), :], (8, LANES)) for r in range(2)]
                    for x, t in enumerate(tiles):
                        q = fields[orb, k, t, :]
                        for r in range(2):
                            acc[r][x] = acc[r][x] - c[r] * q
                for r in range(2):
                    for x, t in enumerate(tiles):
                        fields[orb, 2 * WIDTH + 2 * m + r, t, :] = acc[r][x]
            return 0

        lax.fori_loop(0, WIDTH // 2, rest, 0)
        for n in range(WIDTH):
            acc = None
            for m in range(n + 1):
                c = columns[WIDTH + n * WIDTH + m]
                terms = [c * fields[orb, 2 * WIDTH + m, 8 * x : 8 * x + 8, :] for x in range(SIDE)]
                acc = terms if acc is None else [p + q for p, q in zip(acc, terms)]
            for x in range(SIDE):
                result[orb, n, 8 * x : 8 * x + 8, :] = acc[x]
        stores.append(pltpu.make_async_copy(result.at[orb], out.at[orb], store_sem.at[orb]))
        stores[-1].start()
    for store in stores:
        store.wait()


def per_device(nx, ny, prev, block, seeds, levels, hop, onsite):
    f32, i32 = jnp.float32, jnp.int32
    shape = block.shape
    prev, block = (v.reshape(ORB, WIDTH, ROWS, LANES) for v in (prev, block))
    hop, onsite = hop.transpose(0, 2, 3, 1), onsite.T
    seeds, levels = seeds.reshape(3, ROWS, LANES), levels.reshape(ROWS, LANES)
    hbm, vmem = pl.BlockSpec(memory_space=pltpu.HBM), pl.BlockSpec(memory_space=pltpu.VMEM)
    plane = (2, ORB, WIDTH, 8, LANES)
    dma = pltpu.SemaphoreType.DMA
    product, stats = pl.pallas_call(
        functools.partial(apply_and_reduce, nx, ny),
        out_shape=(jax.ShapeDtypeStruct(block.shape, f32), jax.ShapeDtypeStruct((4, LANES), f32)),
        in_specs=[hbm] * 6,
        out_specs=(hbm, vmem),
        scratch_shapes=[
            pltpu.VMEM((ORB, FIELDS, ROWS + 16, LANES), f32),
            pltpu.VMEM((3, ROWS, LANES), i32),
            pltpu.VMEM((ROWS, LANES), i32),
            pltpu.VMEM(hop.shape, f32),
            pltpu.VMEM(onsite.shape, f32),
            pltpu.VMEM((30, 8, LANES), f32),
            pltpu.VMEM((9, ROWS + 8, LANES), f32),
            pltpu.VMEM((9, ROWS, LANES), f32),
            pltpu.VMEM((9, ROWS, LANES), f32),
            pltpu.VMEM((ORB, ROWS, LANES), f32),
            pltpu.VMEM(plane, f32),
            pltpu.VMEM(plane, f32),
            pltpu.VMEM(plane, f32),
            pltpu.VMEM((8, LANES), i32),
            pltpu.VMEM((8, LANES), i32),
            pltpu.VMEM((8, LANES), i32),
            pltpu.VMEM((group_size(STAGES[0]), 4, LANES), f32),
            pltpu.VMEM((group_size(STAGES[1]), 4, LANES), f32),
            dma((6,)),
            dma((6,)),
            dma((6,)),
            dma((2,)),
            dma((2,)),
            dma,
        ],
        compiler_params=pltpu.CompilerParams(
            collective_id=0, has_side_effects=True, vmem_limit_bytes=58 << 20
        ),
    )(prev, block, seeds, levels, hop, onsite)
    count = float(ORB * ROWS * LANES * nx * ny)
    out, alpha, beta = pl.pallas_call(
        functools.partial(finish, count),
        out_shape=(
            jax.ShapeDtypeStruct(block.shape, f32),
            jax.ShapeDtypeStruct((WIDTH, WIDTH), f32),
            jax.ShapeDtypeStruct((WIDTH, WIDTH), f32),
        ),
        in_specs=[hbm, hbm, hbm, vmem],
        out_specs=(hbm, vmem, vmem),
        scratch_shapes=[
            pltpu.VMEM((ORB, FIELDS, ROWS, LANES), f32),
            pltpu.VMEM((ORB, WIDTH, ROWS, LANES), f32),
            pltpu.VMEM((WIDTH + WIDTH * WIDTH, 8, LANES), f32),
            pltpu.VMEM((2 * WIDTH, 8, LANES), f32),
            dma((ORB, 3)),
            dma((ORB,)),
        ],
        compiler_params=pltpu.CompilerParams(vmem_limit_bytes=58 << 20),
    )(prev, block, product, stats)
    return out.reshape(shape), alpha, beta


def solution(mesh):
    fields = P(None, None, "gx", "gy", None)
    return jax.shard_map(
        functools.partial(per_device, mesh.shape["gx"], mesh.shape["gy"]),
        mesh=mesh,
        in_specs=(fields, fields, P(None, "gx", "gy", None), P("gx", "gy", None), P(), P()),
        out_specs=(fields, P(), P()),
        check_vma=False,
    )
```

time: 393 us -> 43.4 us (0.11)
  blocking collectives: 291 us -> 0 us
  Pallas kernels: 0 us -> 42.6 us
  local copies, waits for them, and re-layouts: 38 us -> 0 us
  starting transfers between devices: 27.2 us -> 0 us
  other arithmetic: 18.6 us -> 0 us
  matrix products: 15.1 us -> 0 us
    psum x3 -> x0, blocking collectives: 291 us -> none  [the longest x1 102 us: per_device(): first = lax.psum(local_inner(basis, product), ('gx', 'gy')) / count]
    pallas_call x0 -> x2, Pallas kernels: none -> 42.6 us  [the longest x1 38.3 us: per_device(): pl.pallas_call(functools.partial(apply_and_reduce, nx, ny), out_shape=(ja...]
    ppermute x6 -> x0, starting transfers between devices: 27.2 us -> none  [the longest x2 10.9 us: extended(): after = lax.ppermute(leading, axis, down)]
    unnamed x171 -> x0, local copies, waits for them, and re-layouts: 17.2 us -> none
    dot_general x25 -> x0, matrix products: 15 us -> none  [the longest x9 6.55 us: local_inner(): lax.dot_general(flat_left, flat_right, (((1,), (1,)), ((), ())), precisio...]
    slice x12 -> x0, local copies, waits for them, and re-layouts: 10.1 us -> none  [the longest x4 4.51 us: local_inner(): flat_left = left[orbit].reshape(left.shape[1], -1)]
    add x8 -> x0, other arithmetic: 8.87 us -> none  [the longest x5 5.72 us: backward(): acc = acc + bonds[left, right][None] * field[left]]
    sub x2 -> x0, other arithmetic: 6.21 us -> none  [the longest x1 3.47 us: per_device(): residual_two = residual_one - combine(basis, second)]
  transfers between devices with their start and end apart: 6 -> 0, of which waited for: 0 -> 0; matrix products, arithmetic and copies ran while one was open for 10% -> 0% of each run, Pallas kernels for 0% -> 0%
where the time goes in v1:
time: 43.4 us; the launch traced here: 43.2 us
  Pallas kernels  42.6 us (98%)
  between operations  0.64 us (1%)
    pallas_call x1, Pallas kernels, per_device(): pl.pallas_call(functools.partial(apply_and_reduce, nx, ny), out_shape=(ja...  38.3 us
    pallas_call x1, Pallas kernels, per_device(): pl.pallas_call(functools.partial(finish, count), out_shape=(jax.ShapeDtyp...  4.3 us

profile of v1, /device:TPU:1, one launch (start us, length us, event | category | flops | bytes accessed | tf_op | source)
XLA Modules:
  0.0 43.2 jit_solution(3838716328502912577)
XLA Ops:
  0.6 38.3 %shard_map.85 = (f32[3,8,64,128]{3,2,1,0:T(8,128)}, f32[4,128]{1,0:T(4,128)}) custom-call(f32[3,8,64,128]{3,2,1,0:T(8,128)} %bitcast.7, f32[3,8,64,128]{3,2,1,0:T(8,128)} %bitcast.9, s32[3,64,128]{2,1,0:T(8,128)} %bitcast.11, s32[64,128]{1,0:T(8,128)} %bitcast.12, f32[3,3,3,16]{3,2,1,0:T(4,128)} %bitcast.13, f32[3,16]{1,0:T(4,128)} %bitcast.14), custom_call_target="tpu_custom_call" | custom-call | tf_op jit(solution)/shard_map/pallas_call | solution.py:397
  38.9 4.3 %shard_map.86 = (f32[3,8,64,128]{3,2,1,0:T(8,128)}, f32[8,8]{1,0:T(8,128)}, f32[8,8]{1,0:T(8,128)}) custom-call(f32[3,8,64,128]{3,2,1,0:T(8,128)} %bitcast.8, f32[3,8,64,128]{3,2,1,0:T(8,128)} %bitcast.10, f32[3,8,64,128]{3,2,1,0:T(8,128)} %get-tuple-element.8.product, f32[4,128]{1,0:T(4,128)} %get-tuple-element.9.stats), custom_call_target="tpu_custom_call" | custom-call | tf_op jit(solution)/shard_map/pallas_call | solution.py:433

commit v2 on v1

--- a/solution.py
+++ b/solution.py
@@ -59,6 +59,16 @@
     return [off for _, _, off in sorted(found, key=lambda t: t[:2])]
 
 
+def moved(pos, dim, steps):
+    new = dict(pos)
+    if dim == "z":
+        z = (pos["zh"] * 2 + pos["zl"] + steps) % 8
+        new["zh"], new["zl"] = z // 2, z % 2
+    else:
+        new[dim] = (pos[dim] + steps) % DIGITS[dim]
+    return device(new)
+
+
 def peer(pos, off):
     return {d: (pos[d] + off[d]) % DIGITS[d] if off.get(d) else pos[d] for d in pos}
 
@@ -78,17 +88,19 @@
     return parts[0]
 
 
-def inner_rows(fields, first, others, lane, sums):
-    def step(x, acc):
-        rows = pl.ds(pl.multiple_of(8 * x + 8, 8), 8)
+def products(fields, first, others, planes, acc):
+    for x in planes:
+        rows = pl.ds(8 * x + 8, 8) if isinstance(x, int) else pl.ds(pl.multiple_of(8 * x + 8, 8), 8)
         for orb in range(ORB):
             left = [fields[orb, first + r, rows, :] for r in range(4)]
             right = [fields[orb, others + s, rows, :] for s in range(8)]
             acc = [acc[r * 8 + s] + left[r] * right[s] for r in range(4) for s in range(8)]
-        return tuple(acc)
-
+    return acc
+
+
+def inner_rows(fields, first, others, lane, sums):
     zero = jnp.zeros((8, LANES), jnp.float32)
-    acc = lax.fori_loop(0, SIDE, step, (zero,) * 32)
+    acc = lax.fori_loop(0, SIDE, lambda x, acc: tuple(products(fields, first, others, (x,), acc)), (zero,) * 32)
     for r in range(4):
         column = jnp.sum(fold_rows(list(acc[r * 8 : r * 8 + 8])), axis=1, keepdims=True)
         sums = jnp.where(iota(1) == lane + r, column, sums)
@@ -102,8 +114,8 @@
 def apply_and_reduce(
     nx, ny, prev, block, seeds, levels, hop, onsite, product, stats,
     fields, seed_v, level_v, hop_v, onsite_v, table, coef_x, coef_y, coef_z, energy,
-    edge_y, halo_x, halo_y, seed_edge, seed_x, seed_y, slots_one, slots_two,
-    load_sem, halo_send, halo_recv, sum_send, sum_recv, store_sem,
+    edge_y, halo_x, halo_y, seed_edge, seed_x, seed_y, slots_one, slots_two, partial, folded,
+    load_sem, halo_send, halo_recv, sum_send, sum_recv, store_sem, known,
 ):
     gx, gy = lax.axis_index("gx"), lax.axis_index("gy")
     right, left = ((gx + 1) % nx, gy), ((gx + nx - 1) % nx, gy)
@@ -112,10 +124,15 @@
     plans = [offsets(dims) for dims in STAGES]
 
     barrier = pltpu.get_barrier_semaphore()
-    partners = [right, left, above, below]
-    partners += [device(peer(pos, off)) for plan in plans for off in plan]
-    for partner in partners:
-        pl.semaphore_signal(barrier, inc=1, device_id=partner, device_id_type=MESH)
+    rings = [moved(pos, dim, k) for dim in ("z", "y") for k in (1, -1, 2, -2)]
+    across = [moved(pos, "x", k) for k in (1, 2, 3)] + [moved(pos, "core", 1)]
+    partners = [right, left, above, below] + rings + across
+
+    def greet(sem, devices):
+        for other in devices:
+            pl.semaphore_signal(sem, inc=1, device_id=other, device_id_type=MESH)
+
+    greet(barrier, partners)
 
     inside = pl.ds(8, ROWS)
     loads = [
@@ -130,6 +147,7 @@
         load.start()
 
     pl.semaphore_wait(barrier, len(partners))
+    greet(known.at[0], rings)
 
     def send(i, src, dst, to):
         return pltpu.make_async_remote_copy(
@@ -164,6 +182,8 @@
     for copy in more:
         copy.start()
     sends += more
+    pl.semaphore_wait(known.at[0], len(rings))
+    greet(known.at[1], across)
 
     for load in loads[2:5]:
         load.wait()
@@ -234,14 +254,40 @@
 
     sums = lax.fori_loop(0, 4, basis_rows, zero)
 
-    for copy in sends:
-        copy.wait_recv()
-    cm = [picked(table[ab], seed_x[...]) for ab in range(9)]
+    for i in (3, 4, 5):
+        sends[i].wait_recv()
     cb = [picked(table[9 + ab], seed_y[...]) for ab in range(9)]
     cf = [picked(table[9 + ab], seed_edge[...]) for ab in range(9)]
+
+    def edges_y(n, _):
+        for a in range(ORB):
+            field = fields.at[a, 2 * WIDTH + n]
+            low, high = field[pl.ds(8, 8, stride=8), :], field[pl.ds(15, 8, stride=8), :]
+            for b in range(ORB):
+                low = low + cb[b * 3 + a] * halo_y[0, b, n]
+                high = high + cf[a * 3 + b] * halo_y[1, b, n]
+            field[pl.ds(8, 8, stride=8), :] = low
+            field[pl.ds(15, 8, stride=8), :] = high
+        return 0
+
+    lax.fori_loop(0, WIDTH, edges_y, 0)
+
+    def inner_planes(i, _):
+        acc = lax.fori_loop(
+            1, SIDE - 1, lambda x, acc: tuple(products(fields, 4 * i, 2 * WIDTH, (x,), acc)), (zero,) * 32
+        )
+        for k in range(32):
+            partial[i, k] = acc[k]
+        return 0
+
+    lax.fori_loop(0, 6, inner_planes, 0)
+
+    for i in (0, 1, 2):
+        sends[i].wait_recv()
+    cm = [picked(table[ab], seed_x[...]) for ab in range(9)]
     cp = [coef_x[ab, ROWS : ROWS + 8, :] for ab in range(9)]
 
-    def edges(n, _):
+    def edges_x(n, _):
         for a in range(ORB):
             field = fields.at[a, 2 * WIDTH + n]
             low, high = field[8:16, :], field[ROWS : ROWS + 8, :]
@@ -250,23 +296,23 @@
                 high = high + cp[a * 3 + b] * halo_x[1, b, n]
             field[8:16, :] = low
             field[ROWS : ROWS + 8, :] = high
-            low, high = field[pl.ds(8, 8, stride=8), :], field[pl.ds(15, 8, stride=8), :]
-            for b in range(ORB):
-                low = low + cb[b * 3 + a] * halo_y[0, b, n]
-                high = high + cf[a * 3 + b] * halo_y[1, b, n]
-            field[pl.ds(8, 8, stride=8), :] = low
-            field[pl.ds(15, 8, stride=8), :] = high
-        return 0
-
-    lax.fori_loop(0, WIDTH, edges, 0)
+        return 0
+
+    lax.fori_loop(0, WIDTH, edges_x, 0)
     keep = pltpu.make_async_copy(fields.at[:, pl.ds(2 * WIDTH, WIDTH), inside, :], product, store_sem)
     keep.start()
 
-    def product_rows(i, sums):
-        return inner_rows(fields, 4 * i, 2 * WIDTH, 4 * i, sums)
-
-    sums = lax.fori_loop(0, 6, product_rows, sums)
+    def outer_planes(i, _):
+        acc = products(fields, 4 * i, 2 * WIDTH, (0, SIDE - 1), [partial[i, k] for k in range(32)])
+        for r in range(4):
+            folded[4 * i + r] = fold_rows(acc[r * 8 : r * 8 + 8])
+        return 0
+
+    lax.fori_loop(0, 6, outer_planes, 0)
+    for k in range(FIELDS):
+        sums = jnp.where(iota(1) == k, jnp.sum(folded[k], axis=1, keepdims=True), sums)
     value = (sums + pltpu.roll(pltpu.roll(sums, 4, axis=0), 64, axis=1))[0:4, :]
+    pl.semaphore_wait(known.at[1], len(across))
     for s, (dims, plan, slots) in enumerate(zip(STAGES, plans, (slots_one, slots_two))):
         me, size = member(pos, dims), group_size(dims)
         slots[me] = value
@@ -418,12 +464,15 @@
             pltpu.VMEM((8, LANES), i32),
             pltpu.VMEM((group_size(STAGES[0]), 4, LANES), f32),
             pltpu.VMEM((group_size(STAGES[1]), 4, LANES), f32),
+            pltpu.VMEM((6, 32, 8, LANES), f32),
+            pltpu.VMEM((FIELDS, 8, LANES), f32),
             dma((6,)),
             dma((6,)),
             dma((6,)),
             dma((2,)),
             dma((2,)),
             dma,
+            pltpu.SemaphoreType.REGULAR((2,)),
         ],
         compiler_params=pltpu.CompilerParams(
             collective_id=0, has_side_effects=True, vmem_limit_bytes=58 << 20

time: 43.4 us -> 40.1 us (0.924)
  Pallas kernels: 42.6 us -> 39.3 us
    pallas_call x1, Pallas kernels: 38.3 us -> 35 us  [per_device(): pl.pallas_call(functools.partial(apply_and_reduce, nx, ny), out_shape=(ja...]
where the time goes in v2:
time: 40.1 us; the launch traced here: 39.9 us
  Pallas kernels  39.3 us (98%)
  between operations  0.64 us (2%)
    pallas_call x1, Pallas kernels, per_device(): pl.pallas_call(functools.partial(apply_and_reduce, nx, ny), out_shape=(ja...  35 us
    pallas_call x1, Pallas kernels, per_device(): pl.pallas_call(functools.partial(finish, count), out_shape=(jax.ShapeDtyp...  4.3 us

profile of v2, /device:TPU:1, one launch (start us, length us, event | category | flops | bytes accessed | tf_op | source)
XLA Modules:
  0.0 39.9 jit_solution(12961920881086265129)
XLA Ops:
  0.6 35.0 %shard_map.85 = (f32[3,8,64,128]{3,2,1,0:T(8,128)}, f32[4,128]{1,0:T(4,128)}) custom-call(f32[3,8,64,128]{3,2,1,0:T(8,128)} %bitcast.7, f32[3,8,64,128]{3,2,1,0:T(8,128)} %bitcast.9, s32[3,64,128]{2,1,0:T(8,128)} %bitcast.11, s32[64,128]{1,0:T(8,128)} %bitcast.12, f32[3,3,3,16]{3,2,1,0:T(4,128)} %bitcast.13, f32[3,16]{1,0:T(4,128)} %bitcast.14), custom_call_target="tpu_custom_call" | custom-call | tf_op jit(solution)/shard_map/pallas_call | solution.py:443
  35.6 4.3 %shard_map.86 = (f32[3,8,64,128]{3,2,1,0:T(8,128)}, f32[8,8]{1,0:T(8,128)}, f32[8,8]{1,0:T(8,128)}) custom-call(f32[3,8,64,128]{3,2,1,0:T(8,128)} %bitcast.8, f32[3,8,64,128]{3,2,1,0:T(8,128)} %bitcast.10, f32[3,8,64,128]{3,2,1,0:T(8,128)} %get-tuple-element.8.product, f32[4,128]{1,0:T(4,128)} %get-tuple-element.9.stats), custom_call_target="tpu_custom_call" | custom-call | tf_op jit(solution)/shard_map/pallas_call | solution.py:482

commit v3 on v2

--- a/solution.py
+++ b/solution.py
@@ -112,10 +112,10 @@
 
 
 def apply_and_reduce(
-    nx, ny, prev, block, seeds, levels, hop, onsite, product, stats,
-    fields, seed_v, level_v, hop_v, onsite_v, table, coef_x, coef_y, coef_z, energy,
+    nx, ny, prev, block, seeds, levels, hop, onsite, fields, stats,
+    seed_v, level_v, hop_v, onsite_v, table, coef_x, coef_y, coef_z, energy,
     edge_y, halo_x, halo_y, seed_edge, seed_x, seed_y, slots_one, slots_two, partial, folded,
-    load_sem, halo_send, halo_recv, sum_send, sum_recv, store_sem, known,
+    load_sem, halo_send, halo_recv, sum_send, sum_recv, known,
 ):
     gx, gy = lax.axis_index("gx"), lax.axis_index("gy")
     right, left = ((gx + 1) % nx, gy), ((gx + nx - 1) % nx, gy)
@@ -299,8 +299,6 @@
         return 0
 
     lax.fori_loop(0, WIDTH, edges_x, 0)
-    keep = pltpu.make_async_copy(fields.at[:, pl.ds(2 * WIDTH, WIDTH), inside, :], product, store_sem)
-    keep.start()
 
     def outer_planes(i, _):
         acc = products(fields, 4 * i, 2 * WIDTH, (0, SIDE - 1), [partial[i, k] for k in range(32)])
@@ -332,7 +330,6 @@
     for s, (dims, slots) in enumerate(zip(STAGES, (slots_one, slots_two))):
         bulk = slots.at[pl.ds(0, group_size(dims) - 1)]
         pltpu.make_async_copy(bulk, bulk, sum_send.at[s]).wait()
-    keep.wait()
 
 
 def wide(matrix):
@@ -346,16 +343,9 @@
 
 
 def finish(
-    count, prev, block, product, stats, out, alpha, beta,
-    fields, result, columns, spread, load_sem, store_sem,
+    count, fields, stats, out, alpha, beta,
+    rest, result, columns, spread, alpha_v, beta_v, store_sem,
 ):
-    loads = []
-    for orb in range(ORB):
-        for i, source in enumerate((prev, block, product)):
-            target = fields.at[orb, pl.ds(i * WIDTH, WIDTH)]
-            loads.append(pltpu.make_async_copy(source.at[orb], target, load_sem.at[orb, i]))
-    for load in loads:
-        load.start()
     row, lane = iota(0), iota(1)
     scaled = stats[...] * (1.0 / count)
     sums = jnp.concatenate([scaled, pltpu.roll(scaled, 64, axis=1)], axis=0)
@@ -369,7 +359,9 @@
         spread[k] = jnp.broadcast_to(coeffs[:, k : k + 1], (8, LANES))
     last = jnp.where(lane < 8, pltpu.roll(first, LANES - 8, axis=1), 0.0)
     unit = jnp.where(row == lane, 1.0, 0.0)
-    alpha[...] = rows_dot(unit, last)[:, 0:WIDTH]
+    alpha_v[...] = rows_dot(unit, last)[:, 0:WIDTH]
+    stores = [pltpu.make_async_copy(alpha_v, alpha, store_sem.at[ORB])]
+    stores[0].start()
     gram = norms + rows_dot(rows_dot(coeffs, metric) - first, coeffs) - rows_dot(coeffs, first)
     for j in range(WIDTH):
         columns[j] = jnp.broadcast_to(gram[:, j : j + 1], (8, LANES))
@@ -391,37 +383,36 @@
             for k in range(j + 1, i):
                 total = total + a[i][k] * inverse[k][j]
             inverse[i][j] = -(total * inverse[i][i])
-    beta[...] = upper[:, 0:WIDTH]
+    beta_v[...] = upper[:, 0:WIDTH]
+    stores.append(pltpu.make_async_copy(beta_v, beta, store_sem.at[ORB + 1]))
+    stores[1].start()
     for i in range(WIDTH):
         for j in range(i + 1):
             columns[WIDTH + i * WIDTH + j] = inverse[i][j]
 
-    stores = []
     for orb in range(ORB):
-        for load in loads[3 * orb : 3 * orb + 3]:
-            load.wait()
-
-        def rest(m, _):
+
+        def residual(m, _):
             for half in range(2):
-                tiles = [pl.ds(8 * (4 * half + x), 8) for x in range(4)]
-                acc = [[fields[orb, 2 * WIDTH + 2 * m + r, t, :] for t in tiles] for r in range(2)]
+                tiles = [8 * (4 * half + x) for x in range(4)]
+                acc = [[fields[orb, 2 * WIDTH + 2 * m + r, pl.ds(t + 8, 8), :] for t in tiles] for r in range(2)]
                 for k in range(2 * WIDTH):
                     c = [jnp.broadcast_to(spread[k, pl.ds(2 * m + r, 1), :], (8, LANES)) for r in range(2)]
                     for x, t in enumerate(tiles):
-                        q = fields[orb, k, t, :]
+                        q = fields[orb, k, pl.ds(t + 8, 8), :]
                         for r in range(2):
                             acc[r][x] = acc[r][x] - c[r] * q
                 for r in range(2):
                     for x, t in enumerate(tiles):
-                        fields[orb, 2 * WIDTH + 2 * m + r, t, :] = acc[r][x]
+                        rest[2 * m + r, pl.ds(t, 8), :] = acc[r][x]
             return 0
 
-        lax.fori_loop(0, WIDTH // 2, rest, 0)
+        lax.fori_loop(0, WIDTH // 2, residual, 0)
         for n in range(WIDTH):
             acc = None
             for m in range(n + 1):
                 c = columns[WIDTH + n * WIDTH + m]
-                terms = [c * fields[orb, 2 * WIDTH + m, 8 * x : 8 * x + 8, :] for x in range(SIDE)]
+                terms = [c * rest[m, 8 * x : 8 * x + 8, :] for x in range(SIDE)]
                 acc = terms if acc is None else [p + q for p, q in zip(acc, terms)]
             for x in range(SIDE):
                 result[orb, n, 8 * x : 8 * x + 8, :] = acc[x]
@@ -437,16 +428,18 @@
     prev, block = (v.reshape(ORB, WIDTH, ROWS, LANES) for v in (prev, block))
     hop, onsite = hop.transpose(0, 2, 3, 1), onsite.T
     seeds, levels = seeds.reshape(3, ROWS, LANES), levels.reshape(ROWS, LANES)
+    operands = (prev, block, seeds, levels, hop, onsite)
+    prev, block, seeds, levels, hop, onsite = (pltpu.with_memory_space_constraint(v, pltpu.HBM) for v in operands)
     hbm, vmem = pl.BlockSpec(memory_space=pltpu.HBM), pl.BlockSpec(memory_space=pltpu.VMEM)
     plane = (2, ORB, WIDTH, 8, LANES)
     dma = pltpu.SemaphoreType.DMA
-    product, stats = pl.pallas_call(
+    every = (ORB, FIELDS, ROWS + 16, LANES)
+    values, stats = pl.pallas_call(
         functools.partial(apply_and_reduce, nx, ny),
-        out_shape=(jax.ShapeDtypeStruct(block.shape, f32), jax.ShapeDtypeStruct((4, LANES), f32)),
+        out_shape=(jax.ShapeDtypeStruct(every, f32), jax.ShapeDtypeStruct((4, LANES), f32)),
         in_specs=[hbm] * 6,
-        out_specs=(hbm, vmem),
+        out_specs=(vmem, vmem),
         scratch_shapes=[
-            pltpu.VMEM((ORB, FIELDS, ROWS + 16, LANES), f32),
             pltpu.VMEM((3, ROWS, LANES), i32),
             pltpu.VMEM((ROWS, LANES), i32),
             pltpu.VMEM(hop.shape, f32),
@@ -471,11 +464,10 @@
             dma((6,)),
             dma((2,)),
             dma((2,)),
-            dma,
             pltpu.SemaphoreType.REGULAR((2,)),
         ],
         compiler_params=pltpu.CompilerParams(
-            collective_id=0, has_side_effects=True, vmem_limit_bytes=58 << 20
+            collective_id=0, has_side_effects=True, vmem_limit_bytes=24 << 20
         ),
     )(prev, block, seeds, levels, hop, onsite)
     count = float(ORB * ROWS * LANES * nx * ny)
@@ -486,18 +478,19 @@
             jax.ShapeDtypeStruct((WIDTH, WIDTH), f32),
             jax.ShapeDtypeStruct((WIDTH, WIDTH), f32),
         ),
-        in_specs=[hbm, hbm, hbm, vmem],
-        out_specs=(hbm, vmem, vmem),
+        in_specs=[vmem, vmem],
+        out_specs=(hbm, hbm, hbm),
         scratch_shapes=[
-            pltpu.VMEM((ORB, FIELDS, ROWS, LANES), f32),
+            pltpu.VMEM((WIDTH, ROWS, LANES), f32),
             pltpu.VMEM((ORB, WIDTH, ROWS, LANES), f32),
             pltpu.VMEM((WIDTH + WIDTH * WIDTH, 8, LANES), f32),
             pltpu.VMEM((2 * WIDTH, 8, LANES), f32),
-            dma((ORB, 3)),
-            dma((ORB,)),
+            pltpu.VMEM((WIDTH, WIDTH), f32),
+            pltpu.VMEM((WIDTH, WIDTH), f32),
+            dma((ORB + 2,)),
         ],
-        compiler_params=pltpu.CompilerParams(vmem_limit_bytes=58 << 20),
-    )(prev, block, product, stats)
+        compiler_params=pltpu.CompilerParams(vmem_limit_bytes=24 << 20),
+    )(values, stats)
     return out.reshape(shape), alpha, beta
 
 

time: 40.1 us -> 38 us (0.948)
  Pallas kernels: 39.3 us -> 37.2 us
    pallas_call x1, Pallas kernels: 4.3 us -> 2.7 us  [per_device(): pl.pallas_call(functools.partial(finish, count), out_shape=(jax.ShapeDtyp...]
    pallas_call x1, Pallas kernels: 35 us -> 34.5 us  [per_device(): pl.pallas_call(functools.partial(apply_and_reduce, nx, ny), out_shape=(ja...]
where the time goes in v3:
time: 38 us; the launch traced here: 37.8 us
  Pallas kernels  37.2 us (98%)
  between operations  0.64 us (2%)
    pallas_call x1, Pallas kernels, per_device(): pl.pallas_call(functools.partial(apply_and_reduce, nx, ny), out_shape=(ja...  34.5 us
    pallas_call x1, Pallas kernels, per_device(): pl.pallas_call(functools.partial(finish, count), out_shape=(jax.ShapeDtyp...  2.7 us

profile of v3, /device:TPU:1, one launch (start us, length us, event | category | flops | bytes accessed | tf_op | source)
XLA Modules:
  0.0 37.8 jit_solution(11151522078674882179)
XLA Ops:
  0.6 34.5 %shard_map.85 = (f32[3,24,80,128]{3,2,1,0:T(8,128)S(1)}, f32[4,128]{1,0:T(4,128)S(1)}) custom-call(f32[3,8,64,128]{3,2,1,0:T(8,128)} %bitcast.7, f32[3,8,64,128]{3,2,1,0:T(8,128)} %bitcast.8, s32[3,64,128]{2,1,0:T(8,128)} %bitcast.9, s32[64,128]{1,0:T(8,128)} %bitcast.10, f32[3,3,3,16]{3,2,1,0:T(4,128)} %bitcast.11, f32[3,16]{1,0:T(4,128)} %bitcast.12), custom_call_target="tpu_custom_call" | custom-call | tf_op jit(solution)/shard_map/pallas_call | solution.py:437
  35.1 2.7 %shard_map.86 = (f32[3,8,64,128]{3,2,1,0:T(8,128)}, f32[8,8]{1,0:T(8,128)}, f32[8,8]{1,0:T(8,128)}) custom-call(f32[3,24,80,128]{3,2,1,0:T(8,128)S(1)} %get-tuple-element.8.fields, f32[4,128]{1,0:T(4,128)S(1)} %get-tuple-element.9.stats), custom_call_target="tpu_custom_call" | custom-call | tf_op jit(solution)/shard_map/pallas_call | solution.py:474

commit v4 on v3

--- a/solution.py
+++ b/solution.py
@@ -88,6 +88,20 @@
     return parts[0]
 
 
+def packed(sums):
+    total = sums
+    for q in (1, 2, 3):
+        total = total + pltpu.roll(pltpu.roll(sums, 8 - 2 * q, axis=0), 32 * q, axis=1)
+    return total[0:2, :]
+
+
+def unpacked(value, spare):
+    spare[0:2, :] = value
+    for q in (1, 2, 3):
+        spare[2 * q : 2 * q + 2, :] = pltpu.roll(value, LANES - 32 * q, axis=1)
+    return spare[...]
+
+
 def products(fields, first, others, planes, acc):
     for x in planes:
         rows = pl.ds(8 * x + 8, 8) if isinstance(x, int) else pl.ds(pl.multiple_of(8 * x + 8, 8), 8)
@@ -112,9 +126,9 @@
 
 
 def apply_and_reduce(
-    nx, ny, prev, block, seeds, levels, hop, onsite, fields, stats,
+    nx, ny, scale, prev, block, seeds, levels, hop, onsite, fields, stats, matrices,
     seed_v, level_v, hop_v, onsite_v, table, coef_x, coef_y, coef_z, energy,
-    edge_y, halo_x, halo_y, seed_edge, seed_x, seed_y, slots_one, slots_two, partial, folded,
+    edge_y, halo_x, halo_y, seed_edge, seed_x, seed_y, slots_one, slots_two, early_one, early_two, partial, folded, spare,
     load_sem, halo_send, halo_recv, sum_send, sum_recv, known,
 ):
     gx, gy = lax.axis_index("gx"), lax.axis_index("gy")
@@ -246,13 +260,34 @@
 
     lax.fori_loop(0, SIDE, own, 0)
 
+    def share(stage, slots, sem, value):
+        me = member(pos, STAGES[stage])
+        slots[me] = value
+        for off in plans[stage]:
+            pltpu.make_async_remote_copy(
+                src_ref=slots.at[me], dst_ref=slots.at[me], send_sem=sum_send.at[sem], recv_sem=sum_recv.at[sem],
+                device_id=device(peer(pos, off)), device_id_type=MESH,
+            ).start()
+
+    def bulk_wait(stage, slots, sems):
+        bulk = slots.at[pl.ds(0, group_size(STAGES[stage]) - 1)]
+        pltpu.make_async_copy(bulk, bulk, sems).wait()
+
+    def gathered(stage, slots, sem):
+        bulk_wait(stage, slots, sum_recv.at[sem])
+        value = slots[0]
+        for k in range(1, group_size(STAGES[stage])):
+            value = value + slots[k]
+        return value
+
     loads[5].wait()
 
     def basis_rows(i, sums):
-        sums = inner_rows(fields, 4 * i, 0, 32 + 4 * i, sums)
-        return inner_rows(fields, 4 * i, WIDTH, 48 + 4 * i, sums)
+        sums = inner_rows(fields, 4 * i, 0, 4 * i, sums)
+        return inner_rows(fields, 4 * i, WIDTH, 16 + 4 * i, sums)
 
     sums = lax.fori_loop(0, 4, basis_rows, zero)
+    early = packed(sums)
 
     for i in (3, 4, 5):
         sends[i].wait_recv()
@@ -281,6 +316,8 @@
         return 0
 
     lax.fori_loop(0, 6, inner_planes, 0)
+    pl.semaphore_wait(known.at[1], len(across))
+    share(0, early_one, 2, early)
 
     for i in (0, 1, 2):
         sends[i].wait_recv()
@@ -307,29 +344,27 @@
         return 0
 
     lax.fori_loop(0, 6, outer_planes, 0)
+    sums = zero
     for k in range(FIELDS):
         sums = jnp.where(iota(1) == k, jnp.sum(folded[k], axis=1, keepdims=True), sums)
-    value = (sums + pltpu.roll(pltpu.roll(sums, 4, axis=0), 64, axis=1))[0:4, :]
-    pl.semaphore_wait(known.at[1], len(across))
-    for s, (dims, plan, slots) in enumerate(zip(STAGES, plans, (slots_one, slots_two))):
-        me, size = member(pos, dims), group_size(dims)
-        slots[me] = value
-        for off in plan:
-            pltpu.make_async_remote_copy(
-                src_ref=slots.at[me], dst_ref=slots.at[me], send_sem=sum_send.at[s], recv_sem=sum_recv.at[s],
-                device_id=device(peer(pos, off)), device_id_type=MESH,
-            ).start()
-        bulk = slots.at[pl.ds(0, size - 1)]
-        pltpu.make_async_copy(bulk, bulk, sum_recv.at[s]).wait()
-        value = slots[0]
-        for k in range(1, size):
-            value = value + slots[k]
-    stats[...] = value
+    share(0, slots_one, 0, packed(sums))
+    share(1, early_two, 3, gathered(0, early_one, 2))
+
+    share(1, slots_two, 1, gathered(0, slots_one, 0))
+
+    both = unpacked(gathered(1, early_two, 3), spare) * scale
+    row, lane = iota(0), iota(1)
+    metric = [jnp.where(lane < 16, both, 0.0), jnp.where(lane < 16, pltpu.roll(both, LANES - 16, axis=1), 0.0)]
+    twice = [jnp.where(row + 8 * i == lane, 2.0, 0.0) - metric[i] for i in range(2)]
+    metric, twice = (jnp.concatenate(m, axis=0) for m in (metric, twice))
+    matrices[0] = twice
+    matrices[1] = 2.0 * twice - rows_dot(rows_dot(twice, metric), twice)
+
+    stats[...] = unpacked(gathered(1, slots_two, 1), spare) * scale
     for copy in sends:
         copy.wait_send()
-    for s, (dims, slots) in enumerate(zip(STAGES, (slots_one, slots_two))):
-        bulk = slots.at[pl.ds(0, group_size(dims) - 1)]
-        pltpu.make_async_copy(bulk, bulk, sum_send.at[s]).wait()
+    for sem, slots in enumerate((slots_one, slots_two, early_one, early_two)):
+        bulk_wait(sem % 2, slots, sum_send.at[sem])
 
 
 def wide(matrix):
@@ -343,18 +378,13 @@
 
 
 def finish(
-    count, fields, stats, out, alpha, beta,
+    fields, stats, matrices, out, alpha, beta,
     rest, result, columns, spread, alpha_v, beta_v, store_sem,
 ):
     row, lane = iota(0), iota(1)
-    scaled = stats[...] * (1.0 / count)
-    sums = jnp.concatenate([scaled, pltpu.roll(scaled, 64, axis=1)], axis=0)
-    first = jnp.where(lane < 16, sums, 0.0)
-    norms = jnp.where(lane < 8, pltpu.roll(sums, LANES - 16, axis=1), 0.0)
-    metric = [jnp.where(lane < 16, pltpu.roll(sums, LANES - at, axis=1), 0.0) for at in (32, 48)]
-    twice = [jnp.where(row + 8 * i == lane, 2.0, 0.0) - metric[i] for i in range(2)]
-    metric, twice = (jnp.concatenate(m, axis=0) for m in (metric, twice))
-    coeffs = rows_dot(first, twice)
+    first = jnp.where(lane < 16, stats[...], 0.0)
+    norms = jnp.where(lane < 8, pltpu.roll(stats[...], LANES - 16, axis=1), 0.0)
+    coeffs = rows_dot(first, matrices[0])
     for k in range(2 * WIDTH):
         spread[k] = jnp.broadcast_to(coeffs[:, k : k + 1], (8, LANES))
     last = jnp.where(lane < 8, pltpu.roll(first, LANES - 8, axis=1), 0.0)
@@ -362,7 +392,7 @@
     alpha_v[...] = rows_dot(unit, last)[:, 0:WIDTH]
     stores = [pltpu.make_async_copy(alpha_v, alpha, store_sem.at[ORB])]
     stores[0].start()
-    gram = norms + rows_dot(rows_dot(coeffs, metric) - first, coeffs) - rows_dot(coeffs, first)
+    gram = norms - rows_dot(rows_dot(first, matrices[1]), first)
     for j in range(WIDTH):
         columns[j] = jnp.broadcast_to(gram[:, j : j + 1], (8, LANES))
 
@@ -434,11 +464,11 @@
     plane = (2, ORB, WIDTH, 8, LANES)
     dma = pltpu.SemaphoreType.DMA
     every = (ORB, FIELDS, ROWS + 16, LANES)
-    values, stats = pl.pallas_call(
-        functools.partial(apply_and_reduce, nx, ny),
-        out_shape=(jax.ShapeDtypeStruct(every, f32), jax.ShapeDtypeStruct((4, LANES), f32)),
+    values, stats, matrices = pl.pallas_call(
+        functools.partial(apply_and_reduce, nx, ny, 1.0 / (ORB * ROWS * LANES * nx * ny)),
+        out_shape=tuple(jax.ShapeDtypeStruct(v, f32) for v in (every, (8, LANES), (2, 2 * WIDTH, LANES))),
         in_specs=[hbm] * 6,
-        out_specs=(vmem, vmem),
+        out_specs=(vmem, vmem, vmem),
         scratch_shapes=[
             pltpu.VMEM((3, ROWS, LANES), i32),
             pltpu.VMEM((ROWS, LANES), i32),
@@ -455,30 +485,32 @@
             pltpu.VMEM((8, LANES), i32),
             pltpu.VMEM((8, LANES), i32),
             pltpu.VMEM((8, LANES), i32),
-            pltpu.VMEM((group_size(STAGES[0]), 4, LANES), f32),
-            pltpu.VMEM((group_size(STAGES[1]), 4, LANES), f32),
+            pltpu.VMEM((group_size(STAGES[0]), 2, LANES), f32),
+            pltpu.VMEM((group_size(STAGES[1]), 2, LANES), f32),
+            pltpu.VMEM((group_size(STAGES[0]), 2, LANES), f32),
+            pltpu.VMEM((group_size(STAGES[1]), 2, LANES), f32),
             pltpu.VMEM((6, 32, 8, LANES), f32),
             pltpu.VMEM((FIELDS, 8, LANES), f32),
+            pltpu.VMEM((8, LANES), f32),
             dma((6,)),
             dma((6,)),
             dma((6,)),
-            dma((2,)),
-            dma((2,)),
+            dma((4,)),
+            dma((4,)),
             pltpu.SemaphoreType.REGULAR((2,)),
         ],
         compiler_params=pltpu.CompilerParams(
             collective_id=0, has_side_effects=True, vmem_limit_bytes=24 << 20
         ),
     )(prev, block, seeds, levels, hop, onsite)
-    count = float(ORB * ROWS * LANES * nx * ny)
     out, alpha, beta = pl.pallas_call(
-        functools.partial(finish, count),
+        finish,
         out_shape=(
             jax.ShapeDtypeStruct(block.shape, f32),
             jax.ShapeDtypeStruct((WIDTH, WIDTH), f32),
             jax.ShapeDtypeStruct((WIDTH, WIDTH), f32),
         ),
-        in_specs=[vmem, vmem],
+        in_specs=[vmem, vmem, vmem],
         out_specs=(hbm, hbm, hbm),
         scratch_shapes=[
             pltpu.VMEM((WIDTH, ROWS, LANES), f32),
@@ -490,7 +522,7 @@
             dma((ORB + 2,)),
         ],
         compiler_params=pltpu.CompilerParams(vmem_limit_bytes=24 << 20),
-    )(values, stats)
+    )(values, stats, matrices)
     return out.reshape(shape), alpha, beta
 
 

time: 38 us -> 37.9 us (level)
  no operation moved by 1% of the time
where the time goes in v4:
time: 37.9 us; the launch traced here: 37.7 us
  Pallas kernels  37.1 us (98%)
  between operations  0.64 us (2%)
    pallas_call x1, Pallas kernels, per_device(): pl.pallas_call(functools.partial(apply_and_reduce, nx, ny, 1.0 / (ORB * R...  34.6 us
    pallas_call x1, Pallas kernels, per_device(): pl.pallas_call(finish, out_shape=(jax.ShapeDtypeStruct(block.shape, f32),...  2.49 us

profile of v4, /device:TPU:1, one launch (start us, length us, event | category | flops | bytes accessed | tf_op | source)
XLA Modules:
  0.0 37.7 jit_solution(12629410437472939196)
XLA Ops:
  0.6 34.6 %shard_map.85 = (f32[3,24,80,128]{3,2,1,0:T(8,128)S(1)}, f32[8,128]{1,0:T(8,128)S(1)}, f32[2,16,128]{2,1,0:T(8,128)S(1)}) custom-call(f32[3,8,64,128]{3,2,1,0:T(8,128)} %bitcast.7, f32[3,8,64,128]{3,2,1,0:T(8,128)} %bitcast.8, s32[3,64,128]{2,1,0:T(8,128)} %bitcast.9, s32[64,128]{1,0:T(8,128)} %bitcast.10, f32[3,3,3,16]{3,2,1,0:T(4,128)} %bitcast.11, ...), custom_call_target="tpu_custom_call" | custom-call | tf_op jit(solution)/shard_map/pallas_call | solution.py:467
  35.3 2.5 %shard_map.86 = (f32[3,8,64,128]{3,2,1,0:T(8,128)}, f32[8,8]{1,0:T(8,128)}, f32[8,8]{1,0:T(8,128)}) custom-call(f32[3,24,80,128]{3,2,1,0:T(8,128)S(1)} %get-tuple-element.9.fields, f32[8,128]{1,0:T(8,128)S(1)} %get-tuple-element.10.stats, f32[2,16,128]{2,1,0:T(8,128)S(1)} %get-tuple-element.11.matrices), custom_call_target="tpu_custom_call" | custom-call | tf_op jit(solution)/shard_map/pallas_call | solution.py:506

commit v5 on v4

--- a/solution.py
+++ b/solution.py
@@ -11,6 +11,7 @@
 MESH = pl.DeviceIdType.MESH
 ORB, WIDTH, SIDE, LANES, KINDS = 3, 8, 8, 128, 16
 ROWS = SIDE * SIDE
+PART = 32
 FIELDS = 3 * WIDTH
 
 DIGITS = {"x": 4, "zh": 4, "y": 8, "zl": 2, "core": 2}
@@ -121,13 +122,22 @@
     return sums
 
 
+def terms(value):
+    found = []
+    for _ in range(3):
+        term = value.astype(jnp.bfloat16)
+        found.append(term)
+        value = value - term.astype(jnp.float32)
+    return found
+
+
 def picked(table, index):
     return jnp.take_along_axis(table, index, axis=1, mode="promise_in_bounds")
 
 
 def apply_and_reduce(
-    nx, ny, scale, prev, block, seeds, levels, hop, onsite, fields, stats, matrices,
-    seed_v, level_v, hop_v, onsite_v, table, coef_x, coef_y, coef_z, energy,
+    nx, ny, scale, prev, block, seeds, levels, hop, onsite, stats, matrices, lines,
+    fields, seed_v, level_v, hop_v, onsite_v, table, coef_x, coef_y, coef_z, energy,
     edge_y, halo_x, halo_y, seed_edge, seed_x, seed_y, slots_one, slots_two, early_one, early_two, partial, folded, spare,
     load_sem, halo_send, halo_recv, sum_send, sum_recv, known,
 ):
@@ -348,9 +358,27 @@
     for k in range(FIELDS):
         sums = jnp.where(iota(1) == k, jnp.sum(folded[k], axis=1, keepdims=True), sums)
     share(0, slots_one, 0, packed(sums))
+
+    flat = fields.reshape(ORB, FIELDS * (ROWS + 16), LANES)
+    padding = jnp.zeros((PART - FIELDS, LANES), jnp.float32)
+
+    def line_terms(orb):
+        def step(x, _):
+            for y in range(8):
+                value = flat[orb, pl.ds(8 * x + 8 + y, FIELDS, stride=ROWS + 16), :]
+                value = jnp.concatenate([value, padding], axis=0)
+                for i, term in enumerate(terms(value)):
+                    lines[orb, 8 * x + y, i * PART : (i + 1) * PART, :] = term
+            return 0
+
+        lax.fori_loop(0, SIDE, step, 0)
+
+    line_terms(0)
     share(1, early_two, 3, gathered(0, early_one, 2))
 
     share(1, slots_two, 1, gathered(0, slots_one, 0))
+    line_terms(1)
+    line_terms(2)
 
     both = unpacked(gathered(1, early_two, 3), spare) * scale
     row, lane = iota(0), iota(1)
@@ -378,15 +406,13 @@
 
 
 def finish(
-    fields, stats, matrices, out, alpha, beta,
-    rest, result, columns, spread, alpha_v, beta_v, store_sem,
+    lines, stats, matrices, out, alpha, beta,
+    result, columns, alpha_v, beta_v, store_sem,
 ):
     row, lane = iota(0), iota(1)
     first = jnp.where(lane < 16, stats[...], 0.0)
     norms = jnp.where(lane < 8, pltpu.roll(stats[...], LANES - 16, axis=1), 0.0)
     coeffs = rows_dot(first, matrices[0])
-    for k in range(2 * WIDTH):
-        spread[k] = jnp.broadcast_to(coeffs[:, k : k + 1], (8, LANES))
     last = jnp.where(lane < 8, pltpu.roll(first, LANES - 8, axis=1), 0.0)
     unit = jnp.where(row == lane, 1.0, 0.0)
     alpha_v[...] = rows_dot(unit, last)[:, 0:WIDTH]
@@ -416,36 +442,27 @@
     beta_v[...] = upper[:, 0:WIDTH]
     stores.append(pltpu.make_async_copy(beta_v, beta, store_sem.at[ORB + 1]))
     stores[1].start()
-    for i in range(WIDTH):
-        for j in range(i + 1):
-            columns[WIDTH + i * WIDTH + j] = inverse[i][j]
+    weights = jnp.zeros((8, LANES), jnp.float32)
+    for m in range(WIDTH):
+        column = jnp.zeros((8, LANES), jnp.float32)
+        for n in range(m, WIDTH):
+            column = jnp.where(row == n, inverse[n][m], column)
+        weights = weights - column * jnp.broadcast_to(coeffs[m : m + 1, :], (8, LANES))
+        weights = jnp.where(lane == 2 * WIDTH + m, column, weights)
+    high, middle, low = (term.astype(jnp.float32) for term in terms(weights))
+    shifted = [[pltpu.roll(t, PART * i, axis=1) if i else t for i in range(c)] for t, c in ((high, 3), (middle, 2), (low, 1))]
+    matrix = jnp.concatenate([sum(group[1:], group[0]) for group in shifted], axis=0).astype(jnp.bfloat16)
+    matrix = matrix[:, : 3 * PART]
 
     for orb in range(ORB):
 
-        def residual(m, _):
-            for half in range(2):
-                tiles = [8 * (4 * half + x) for x in range(4)]
-                acc = [[fields[orb, 2 * WIDTH + 2 * m + r, pl.ds(t + 8, 8), :] for t in tiles] for r in range(2)]
-                for k in range(2 * WIDTH):
-                    c = [jnp.broadcast_to(spread[k, pl.ds(2 * m + r, 1), :], (8, LANES)) for r in range(2)]
-                    for x, t in enumerate(tiles):
-                        q = fields[orb, k, pl.ds(t + 8, 8), :]
-                        for r in range(2):
-                            acc[r][x] = acc[r][x] - c[r] * q
-                for r in range(2):
-                    for x, t in enumerate(tiles):
-                        rest[2 * m + r, pl.ds(t, 8), :] = acc[r][x]
-            return 0
-
-        lax.fori_loop(0, WIDTH // 2, residual, 0)
-        for n in range(WIDTH):
-            acc = None
-            for m in range(n + 1):
-                c = columns[WIDTH + n * WIDTH + m]
-                terms = [c * rest[m, 8 * x : 8 * x + 8, :] for x in range(SIDE)]
-                acc = terms if acc is None else [p + q for p, q in zip(acc, terms)]
-            for x in range(SIDE):
-                result[orb, n, 8 * x : 8 * x + 8, :] = acc[x]
+        for x in range(SIDE):
+            for y in range(0, 8, 2):
+                pair = jnp.concatenate([lines[orb, 8 * x + y + i] for i in range(2)], axis=1)
+                got = jnp.dot(matrix, pair, preferred_element_type=jnp.float32)
+                got = got[0:8] + got[8:16] + got[16:24]
+                for i in range(2):
+                    result[orb, pl.ds(8 * x + y + i, 8, stride=ROWS), :] = got[:, i * LANES : (i + 1) * LANES]
         stores.append(pltpu.make_async_copy(result.at[orb], out.at[orb], store_sem.at[orb]))
         stores[-1].start()
     for store in stores:
@@ -463,13 +480,14 @@
     hbm, vmem = pl.BlockSpec(memory_space=pltpu.HBM), pl.BlockSpec(memory_space=pltpu.VMEM)
     plane = (2, ORB, WIDTH, 8, LANES)
     dma = pltpu.SemaphoreType.DMA
-    every = (ORB, FIELDS, ROWS + 16, LANES)
-    values, stats, matrices = pl.pallas_call(
+    stats, matrices, lines = pl.pallas_call(
         functools.partial(apply_and_reduce, nx, ny, 1.0 / (ORB * ROWS * LANES * nx * ny)),
-        out_shape=tuple(jax.ShapeDtypeStruct(v, f32) for v in (every, (8, LANES), (2, 2 * WIDTH, LANES))),
+        out_shape=tuple(jax.ShapeDtypeStruct(v, f32) for v in ((8, LANES), (2, 2 * WIDTH, LANES)))
+        + (jax.ShapeDtypeStruct((ORB, ROWS, 3 * PART, LANES), jnp.bfloat16),),
         in_specs=[hbm] * 6,
         out_specs=(vmem, vmem, vmem),
         scratch_shapes=[
+            pltpu.VMEM((ORB, FIELDS, ROWS + 16, LANES), f32),
             pltpu.VMEM((3, ROWS, LANES), i32),
             pltpu.VMEM((ROWS, LANES), i32),
             pltpu.VMEM(hop.shape, f32),
@@ -506,23 +524,21 @@
     out, alpha, beta = pl.pallas_call(
         finish,
         out_shape=(
-            jax.ShapeDtypeStruct(block.shape, f32),
+            jax.ShapeDtypeStruct((ORB, WIDTH * ROWS, LANES), f32),
             jax.ShapeDtypeStruct((WIDTH, WIDTH), f32),
             jax.ShapeDtypeStruct((WIDTH, WIDTH), f32),
         ),
         in_specs=[vmem, vmem, vmem],
         out_specs=(hbm, hbm, hbm),
         scratch_shapes=[
-            pltpu.VMEM((WIDTH, ROWS, LANES), f32),
-            pltpu.VMEM((ORB, WIDTH, ROWS, LANES), f32),
-            pltpu.VMEM((WIDTH + WIDTH * WIDTH, 8, LANES), f32),
-            pltpu.VMEM((2 * WIDTH, 8, LANES), f32),
+            pltpu.VMEM((ORB, WIDTH * ROWS, LANES), f32),
+            pltpu.VMEM((WIDTH, 8, LANES), f32),
             pltpu.VMEM((WIDTH, WIDTH), f32),
             pltpu.VMEM((WIDTH, WIDTH), f32),
             dma((ORB + 2,)),
         ],
         compiler_params=pltpu.CompilerParams(vmem_limit_bytes=24 << 20),
-    )(values, stats, matrices)
+    )(lines, stats, matrices)
     return out.reshape(shape), alpha, beta
 
 

time: 37.9 us -> 37.4 us (0.987)
  Pallas kernels: 37.1 us -> 36.7 us
where the time goes in v5:
time: 37.4 us; the launch traced here: 37.3 us
  Pallas kernels  36.7 us (98%)
  between operations  0.64 us (2%)
    pallas_call x1, Pallas kernels, per_device(): pl.pallas_call(functools.partial(apply_and_reduce, nx, ny, 1.0 / (ORB * R...  34.5 us
    pallas_call x1, Pallas kernels, per_device(): pl.pallas_call(finish, out_shape=(jax.ShapeDtypeStruct((ORB, WIDTH * ROWS...  2.15 us

profile of v5, /device:TPU:1, one launch (start us, length us, event | category | flops | bytes accessed | tf_op | source)
XLA Modules:
  0.0 37.3 jit_solution(7076496530617029932)
XLA Ops:
  0.6 34.5 %shard_map.85 = (f32[8,128]{1,0:T(8,128)S(1)}, f32[2,16,128]{2,1,0:T(8,128)S(1)}, bf16[3,64,96,128]{3,2,1,0:T(8,128)(2,1)S(1)}) custom-call(f32[3,8,64,128]{3,2,1,0:T(8,128)} %bitcast.7, f32[3,8,64,128]{3,2,1,0:T(8,128)} %bitcast.8, s32[3,64,128]{2,1,0:T(8,128)} %bitcast.9, s32[64,128]{1,0:T(8,128)} %bitcast.10, f32[3,3,3,16]{3,2,1,0:T(4,128)} %bitcast.11, ...), custom_call_target="tpu_custom_call" | custom-call | tf_op jit(solution)/shard_map/pallas_call | solution.py:483
  35.2 2.1 %shard_map.86 = (f32[3,512,128]{2,1,0:T(8,128)}, f32[8,8]{1,0:T(8,128)}, f32[8,8]{1,0:T(8,128)}) custom-call(bf16[3,64,96,128]{3,2,1,0:T(8,128)(2,1)S(1)} %get-tuple-element.9.lines, f32[8,128]{1,0:T(8,128)S(1)} %get-tuple-element.10.stats, f32[2,16,128]{2,1,0:T(8,128)S(1)} %get-tuple-element.11.matrices), custom_call_target="tpu_custom_call" | custom-call | tf_op jit(solution)/shard_map/pallas_call | solution.py:524

commit v6 on v5

--- a/solution.py
+++ b/solution.py
@@ -345,7 +345,8 @@
             field[ROWS : ROWS + 8, :] = high
         return 0
 
-    lax.fori_loop(0, WIDTH, edges_x, 0)
+    for n in range(WIDTH):
+        edges_x(n, 0)
 
     def outer_planes(i, _):
         acc = products(fields, 4 * i, 2 * WIDTH, (0, SIDE - 1), [partial[i, k] for k in range(32)])
@@ -353,7 +354,8 @@
             folded[4 * i + r] = fold_rows(acc[r * 8 : r * 8 + 8])
         return 0
 
-    lax.fori_loop(0, 6, outer_planes, 0)
+    for i in range(6):
+        outer_planes(i, 0)
     sums = zero
     for k in range(FIELDS):
         sums = jnp.where(iota(1) == k, jnp.sum(folded[k], axis=1, keepdims=True), sums)

time: 37.4 us -> 37.4 us (level)
  no operation moved by 1% of the time
where the time goes in v6:
time: 37.4 us; the launch traced here: 37.3 us
  Pallas kernels  36.7 us (98%)
  between operations  0.64 us (2%)
    pallas_call x1, Pallas kernels, per_device(): pl.pallas_call(functools.partial(apply_and_reduce, nx, ny, 1.0 / (ORB * R...  34.5 us
    pallas_call x1, Pallas kernels, per_device(): pl.pallas_call(finish, out_shape=(jax.ShapeDtypeStruct((ORB, WIDTH * ROWS...  2.15 us

profile of v6, /device:TPU:1, one launch (start us, length us, event | category | flops | bytes accessed | tf_op | source)
XLA Modules:
  0.0 37.3 jit_solution(17431069919777022437)
XLA Ops:
  0.6 34.5 %shard_map.85 = (f32[8,128]{1,0:T(8,128)S(1)}, f32[2,16,128]{2,1,0:T(8,128)S(1)}, bf16[3,64,96,128]{3,2,1,0:T(8,128)(2,1)S(1)}) custom-call(f32[3,8,64,128]{3,2,1,0:T(8,128)} %bitcast.7, f32[3,8,64,128]{3,2,1,0:T(8,128)} %bitcast.8, s32[3,64,128]{2,1,0:T(8,128)} %bitcast.9, s32[64,128]{1,0:T(8,128)} %bitcast.10, f32[3,3,3,16]{3,2,1,0:T(4,128)} %bitcast.11, ...), custom_call_target="tpu_custom_call" | custom-call | tf_op jit(solution)/shard_map/pallas_call | solution.py:485
  35.2 2.1 %shard_map.86 = (f32[3,512,128]{2,1,0:T(8,128)}, f32[8,8]{1,0:T(8,128)}, f32[8,8]{1,0:T(8,128)}) custom-call(bf16[3,64,96,128]{3,2,1,0:T(8,128)(2,1)S(1)} %get-tuple-element.9.lines, f32[8,128]{1,0:T(8,128)S(1)} %get-tuple-element.10.stats, f32[2,16,128]{2,1,0:T(8,128)S(1)} %get-tuple-element.11.matrices), custom_call_target="tpu_custom_call" | custom-call | tf_op jit(solution)/shard_map/pallas_call | solution.py:526
